TPU v7x, 512 devices: a whole 4x8x8 slice. The times are simulated.
512 devices in a mesh: src: 16 (over z_hi, x, core), rows: 32 (over z_lo, y).
Axes of the slice: x: 4, y: 8, z: 8 (z_hi: 2, z_lo: 4; z = z_hi * 4 + z_lo), core: 2. Of those that a mesh axis runs over, the one named last changes fastest.
Arguments:
- mask_param: float32 [512, 8192], P('rows'), may hold values from -6 to 6
- target: int32 [512, 8192], P('rows', 'src'), may hold values 0 or 1
- source_weight: float32 [16], replicated, may hold values from 0.25 to 4
- row_shift: int32 [16], replicated, may hold values from -8 to 8
- col_shift: int32 [16], replicated, may hold values from -32 to 32
Outputs:
- mask_grad: float32 [512, 8192], P('rows', 'src')
All inputs are finite; a program needn't handle non-finite values. No bound on the sum of `target` on one device may be relied on, other than what follows from the above.
Results may differ from a plain program's by a relative error of at most 0.0003.
Values sent between devices are 32-bit elements; how exact they have to be, the bound alone decides.
No kernel may reach another device: no remote copies, remote signals or barrier semaphores. Data moves between devices by JAX's collectives and lax.ppermute only.
A program may use at most 64 MiB of HBM per device.

v0:
```python
import math

import jax
import jax.numpy as jnp
import numpy as np
from jax import lax
from jax.experimental import pallas as pl
from jax.experimental.pallas import tpu as pltpu
from jax.sharding import Mesh
from jax.sharding import PartitionSpec as P


steepness = 250.0
threshold_level = 0.25
loss_weight = 8.0
highest = lax.Precision.HIGHEST
KERNELS = True

NR = 512
NC = 8192
KR = 32
KC = 128
MC = 256
HALF = KC // 2
SHARE = 512
BLOCKS = NC // SHARE
ROWS = 16
ROW_BLOCKS = NR // ROWS
POINTS = 16
NEAR = 8
STEP = MC // BLOCKS
LINES = ROWS + 1
UNIT = 1.0 / math.sqrt(NR * NC)


def f32(table):
    return np.ascontiguousarray(np.asarray(table, dtype=np.float32))


def wave(frequency, position, period):
    angle = (np.outer(frequency, position) % period) * (2.0 * np.pi / period)
    return np.cos(angle), np.sin(angle)


def column_table():
    cos, sin = wave(np.arange(HALF + 1), np.arange(SHARE), NC)
    table = np.zeros((2 * KC, SHARE))
    table[:HALF] = cos[:HALF]
    table[HALF] = cos[HALF]
    table[HALF + 1 : KC] = -sin[1:HALF]
    table[KC] = -sin[HALF]
    return f32(table[: KC + 8])


def turn_tables():
    cos, sin = wave(np.arange(BLOCKS), np.arange(HALF), BLOCKS)
    return f32(np.concatenate([cos, cos], axis=1)), f32(np.concatenate([sin, -sin], axis=1))


def spread_table():
    table = np.zeros((KC, 2 * KC))
    for frequency in range(-HALF, HALF):
        size, at = abs(frequency), frequency + HALF
        table[size, at] = 1.0
        if 0 < size < HALF:
            table[HALF + size, KC + at] = 1.0 if frequency > 0 else -1.0
    return f32(table)


def band_tables():
    frequency = np.arange(KR) - KR // 2
    rows = np.concatenate(wave(frequency, np.arange(NR), NR)) * (UNIT * UNIT)
    inner = np.zeros((2 * KR, KC))
    inner[:, :ROWS] = np.concatenate(wave(frequency, np.arange(ROWS), NR)) * (UNIT * UNIT)
    outer = np.concatenate(wave(frequency, np.arange(ROW_BLOCKS) * ROWS, NR))
    return f32(rows), f32(inner), f32(outer)


def own_row_table():
    cos, sin = wave(np.arange(NR), np.arange(KR) - KR // 2, NR)
    cos = cos.reshape(ROW_BLOCKS, ROWS, KR)
    sin = sin.reshape(ROW_BLOCKS, ROWS, KR)
    turn = np.concatenate(
        [np.concatenate([cos, -sin], axis=2), np.concatenate([sin, cos], axis=2)], axis=1
    )
    return f32(turn)


def sample_table():
    cos, sin = wave(np.arange(KC) - HALF, np.arange(MC), MC)
    return np.block([[cos, sin], [-sin, cos]])


def interpolation_table():
    place = (np.arange(MC)[:, None] * (NC // MC) - np.arange(SHARE)[None, :]) % NC
    total = np.ones_like(place, dtype=np.float64)
    for k in range(1, HALF + 1):
        total += 2.0 * np.cos(((place * k) % NC) * (2.0 * np.pi / NC))
    return total / MC


def fold_tables():
    columns = np.zeros((KC, 2 * KC))
    for frequency in range(-HALF, HALF):
        at, size = frequency + HALF, abs(frequency)
        columns[at, size] = 1.0
        if size > 0:
            columns[at, HALF + size] = -1.0 if frequency > 0 else 1.0
    columns[0, KC] = 1.0
    columns[0, HALF] = 1.0
    rows = np.zeros((KC, 2 * KR))
    for frequency in range(-KR // 2, KR // 2):
        at, size = frequency + KR // 2, abs(frequency)
        rows[size, at] = 1.0
        if size > 0:
            rows[KR // 2 + size, KR + at] = float(np.sign(frequency))
    pick = np.zeros((8, KC))
    pick[1, 0] = 1.0
    return f32(columns), f32(rows), f32(pick)


def final_tables():
    cos, sin = wave(np.arange(NR), np.arange(KR // 2 + 1), NR)
    rows = np.zeros((NR, KC))
    rows[:, : KR // 2 + 1] = cos * UNIT
    rows[:, KR // 2 + 1 : KR + 1] = sin[:, 1:] * UNIT
    cos_y, sin_y = wave(np.arange(HALF + 1), np.arange(SHARE), NC)
    columns = np.concatenate([cos_y, sin_y[1:HALF]])
    return f32(rows.reshape(ROW_BLOCKS, ROWS, KC)), f32(columns), f32(sin_y[HALF:])


def dot(left, right):
    return jnp.dot(left, right, precision=highest, preferred_element_type=jnp.float32)


def dot_nt(left, right, precision=highest):
    return lax.dot_general(
        left, right, (((1,), (1,)), ((), ())), precision=precision, preferred_element_type=jnp.float32
    )


def split(values):
    high = values.astype(jnp.bfloat16)
    return high, (values - high.astype(jnp.float32)).astype(jnp.bfloat16)


def dot3_nt(left, right):
    high, low = split(left)
    right_high, right_low = split(right)
    one = lambda a, b: dot_nt(a, b, None)
    return one(high, right_high) + (one(high, right_low) + one(low, right_high))


def dot_tn(left, right):
    return lax.dot_general(
        left, right, (((0,), (0,)), ((), ())), precision=highest, preferred_element_type=jnp.float32
    )


def logistic(values):
    return 1.0 / (1.0 + jnp.exp(-values))


def roll(values, shift):
    if KERNELS:
        return pltpu.roll(values, shift, axis=1)
    return jnp.roll(values, shift, axis=1)


def lanes(shape):
    return lax.broadcasted_iota(jnp.int32, shape, 1)


def columns_math(mask, base, turn_cos, turn_sin, pick):
    stacked = jnp.concatenate(
        [logistic(mask[:, SHARE * b : SHARE * (b + 1)]) for b in range(BLOCKS)], axis=0
    )
    parts = dot_nt(stacked, base)
    main = jnp.zeros((ROWS, KC), jnp.float32)
    edge = jnp.zeros((ROWS, 8), jnp.float32)
    for b in range(BLOCKS):
        part = parts[ROWS * b : ROWS * (b + 1)]
        first = part[:, :KC]
        main = main + first * turn_cos[b : b + 1] + roll(first, HALF) * turn_sin[b : b + 1]
        edge = edge + part[:, KC:]
    edge = jnp.concatenate([edge, jnp.zeros((KC - ROWS, 8), jnp.float32)], axis=0)
    return main, dot_nt(pick[:, :8], edge)[1:2]


def pupil(row_shift, col_shift):
    radius_rows = KR // 4
    radius_cols = KC // 4
    fr = lax.broadcasted_iota(jnp.int32, (KR, KC), 0) - KR // 2 + row_shift
    fc = lanes((KR, KC)) - HALF + col_shift
    limit_value = (radius_rows * radius_cols) ** 2
    inside = fr * fr * (radius_cols * radius_cols) + fc * fc * (radius_rows * radius_rows)
    return (inside <= limit_value).astype(jnp.float32)


def middle_math(
    shifts,
    weight,
    row_shift,
    col_shift,
    main,
    edge,
    target,
    turn,
    rows,
    inner,
    outer,
    spread,
    to_samples,
    interpolate,
    fold_columns,
    fold_rows,
    pick,
):
    both = dot(dot(rows, main), spread)
    inside = dot_nt(inner, edge)
    in_cos, in_sin = inside[:KR], inside[KR:]
    out_cos, out_sin = outer[:KR], outer[KR:]
    edge_cos = jnp.sum(out_cos * in_cos - out_sin * in_sin, axis=1, keepdims=True)
    edge_sin = jnp.sum(out_sin * in_cos + out_cos * in_sin, axis=1, keepdims=True)
    edge_column = jnp.concatenate([edge_cos, edge_sin], axis=0)
    real = both[:, :KC]
    imag = both[:, KC:] - jnp.where(lanes((2 * KR, KC)) == 0, edge_column, 0.0)
    band_real = real[:KR] + imag[KR:]
    band_imag = imag[:KR] - real[KR:]

    opened = [pupil(row_shift[s], col_shift[s]) for s in range(POINTS)]
    masked = jnp.concatenate(
        [
            jnp.concatenate([band_real * opened[s], band_imag * opened[s]], axis=0)
            for s in range(POINTS)
        ],
        axis=1,
    )
    head = dot(turn, masked)
    head = jnp.concatenate(
        [
            jnp.concatenate(
                [head[:ROWS, KC * s : KC * (s + 1)], head[ROWS:, KC * s : KC * (s + 1)]], axis=1
            )
            for s in range(POINTS)
        ],
        axis=0,
    )
    field = dot(head, to_samples)
    samples = jnp.zeros((ROWS, MC), jnp.float32)
    total = 0.0
    for s in range(POINTS):
        now = field[ROWS * s : ROWS * (s + 1)]
        samples = samples + weight[s] * (now[:, :MC] * now[:, :MC] + now[:, MC:] * now[:, MC:])
        total = total + weight[s]
    share = 1.0 / jnp.full((ROWS, MC), total, jnp.float32)
    samples = samples * share
    near = jnp.concatenate(
        [roll(samples, (MC - shifts[j]) & (MC - 1)) for j in range(NEAR)], axis=0
    )
    intensity = dot(near, interpolate)
    resist = logistic(steepness * (intensity - threshold_level))
    slope = (
        2.0
        * loss_weight
        * (resist - target.astype(jnp.float32))
        * steepness
        * resist
        * (1.0 - resist)
    )
    lows = dot3_nt(slope, interpolate)
    low = roll(lows[:ROWS], shifts[0])
    for j in range(1, NEAR):
        low = low + roll(lows[ROWS * j : ROWS * (j + 1)], shifts[j])
    low = low * share * (2.0 * UNIT)
    wide = jnp.concatenate([low, low], axis=1)
    scaled = jnp.concatenate(
        [(weight[s] * wide) * field[ROWS * s : ROWS * (s + 1)] for s in range(POINTS)], axis=0
    )
    back = dot3_nt(scaled, to_samples)
    back = jnp.concatenate(
        [
            jnp.concatenate(
                [back[ROWS * s : ROWS * (s + 1), :KC], back[ROWS * s : ROWS * (s + 1), KC:]], axis=0
            )
            for s in range(POINTS)
        ],
        axis=1,
    )
    spectra = dot_tn(turn, back)
    adjoint_real = jnp.zeros((KR, KC), jnp.float32)
    adjoint_imag = jnp.zeros((KR, KC), jnp.float32)
    for s in range(POINTS):
        now = spectra[:, KC * s : KC * (s + 1)]
        adjoint_real = adjoint_real + opened[s] * now[:KR]
        adjoint_imag = adjoint_imag + opened[s] * now[KR:]
    folded = dot(jnp.concatenate([adjoint_real, adjoint_imag], axis=0), fold_columns)
    real, imag = folded[:KR], folded[KR:]
    even = lanes((KR, 2 * KC)) <= HALF
    kinds = jnp.concatenate([jnp.where(even, real, imag), jnp.where(even, -imag, real)], axis=0)
    packed = dot(fold_rows, kinds)
    last = dot_nt(pick, packed[:, KC:])
    return jnp.concatenate([packed[:KR, :KC], packed[KR : KR + 8, :KC] + last], axis=0)


def final_math(total, mask, rows, turn_cos, turn_sin, columns, last_column):
    part = dot(rows[:, :40], total)
    edge = jnp.sum(rows * total[KR + 1 : KR + 2], axis=1, keepdims=True)
    turned = part * turn_cos + roll(part, HALF) * turn_sin
    grad = dot(turned, columns) + edge * last_column
    opening = logistic(mask)
    return grad * opening * (1.0 - opening)


VMEM = pl.BlockSpec(memory_space=pltpu.VMEM)
SMEM = pl.BlockSpec(memory_space=pltpu.SMEM)


def call(body, outputs, scalars, arrays):
    arrays = [pltpu.with_memory_space_constraint(array, pltpu.VMEM) for array in arrays]
    return pl.pallas_call(
        body,
        in_specs=[SMEM] * len(scalars) + [VMEM] * len(arrays),
        out_specs=jax.tree.map(lambda _: VMEM, outputs),
        out_shape=outputs,
    )(*scalars, *arrays)


def plain(*shape):
    return jax.ShapeDtypeStruct(shape, jnp.float32)


def pick_block(table, index):
    return lax.dynamic_index_in_dim(jnp.asarray(table), index, 0, False)


def columns_part(row_index, mask_param):
    tables = (column_table(), *turn_tables(), fold_tables()[2])
    turn = own_row_table()
    if not KERNELS:
        message = jnp.concatenate(columns_math(mask_param, *tables))
        return repeated(message, ROW_BLOCKS), pick_block(turn, row_index)

    def kernel(place, mask_ref, turn_ref, *refs):
        *refs, out_ref, own_ref = refs
        own_ref[...] = turn_ref[0]
        main, edge = columns_math(mask_ref[...], *[ref[...] for ref in refs])
        for b in range(ROW_BLOCKS):
            out_ref[LINES * b : LINES * b + ROWS] = main
            out_ref[LINES * b + ROWS : LINES * (b + 1)] = edge

    full = lambda shape: pl.BlockSpec(shape, lambda i, place: (0,) * len(shape))
    outputs = (
        pltpu.VMEM((ROW_BLOCKS * LINES, KC), jnp.float32),
        pltpu.VMEM(turn.shape[1:], jnp.float32),
    )
    sent, own = pl.pallas_call(
        kernel,
        grid_spec=pltpu.PrefetchScalarGridSpec(
            num_scalar_prefetch=1,
            grid=(1,),
            in_specs=[
                full(mask_param.shape),
                pl.BlockSpec((1, *turn.shape[1:]), lambda i, place: (place[0], 0, 0)),
                *[full(table.shape) for table in tables],
            ],
            out_specs=tuple(full(output.shape) for output in outputs),
        ),
        out_shape=outputs,
        name="columns_part",
    )(row_index.reshape(1), mask_param, turn, *tables)
    return sent.reshape(ROW_BLOCKS, 1, LINES * KC), own


def repeated(values, count):
    return jnp.broadcast_to(values[None], (count, *values.shape))


def middle_part(shifts, weight, row_shift, col_shift, heard, targets, turn):
    heard = heard.reshape(ROW_BLOCKS * LINES, KC)
    targets = [target.reshape(-1, SHARE) for target in targets]
    arrays = (
        heard,
        *targets,
        turn,
        *band_tables(),
        spread_table(),
        f32(sample_table()),
        f32(interpolation_table()),
        *fold_tables(),
    )
    scalars = (shifts, weight, row_shift, col_shift)
    if not KERNELS:
        lines = heard.reshape(ROW_BLOCKS, LINES, KC)
        main, edge = lines[:, :ROWS].reshape(NR, KC), lines[:, ROWS]
        target = jnp.concatenate(targets)
        return repeated(middle_math(*scalars, main, edge, target, *arrays[1 + len(targets) :]), 8)

    def kernel(shift_ref, weight_ref, row_ref, col_ref, heard_ref, *refs):
        *refs, out_ref = refs
        main = jnp.concatenate(
            [heard_ref[LINES * b : LINES * b + ROWS] for b in range(ROW_BLOCKS)], axis=0
        )
        edge = heard_ref[pl.ds(ROWS, ROW_BLOCKS, stride=LINES)]
        values = [ref[...] for ref in refs]
        target = jnp.concatenate(values[: len(targets)], axis=0)
        message = middle_math(
            shift_ref, weight_ref, row_ref, col_ref, main, edge, target, *values[len(targets) :]
        )
        for b in range(8):
            out_ref[b] = message

    return call(kernel, plain(8, 40, KC), scalars, arrays)


def repeat_sum(received):
    if not KERNELS:
        return jnp.broadcast_to(jnp.sum(received, axis=0)[None], received.shape)

    def kernel(in_ref, out_ref):
        total = in_ref[0]
        for b in range(1, received.shape[0]):
            total = total + in_ref[b]
        for b in range(received.shape[0]):
            out_ref[b] = total

    return call(kernel, pltpu.VMEM(received.shape, jnp.float32), (), (received,))


def final_part(src_index, row_index, received, mask_param):
    rows, columns, last_column = final_tables()
    arrays = (
        received,
        lax.dynamic_slice_in_dim(mask_param, src_index * SHARE, SHARE, 1),
        pick_block(rows, row_index),
        *[pick_block(table.reshape(BLOCKS, 1, KC), src_index) for table in turn_tables()],
        columns,
        last_column,
    )
    if not KERNELS:
        return final_math(jnp.sum(received, axis=0), *arrays[1:])

    def kernel(in_ref, *refs):
        *refs, out_ref = refs
        total = in_ref[0]
        for b in range(1, received.shape[0]):
            total = total + in_ref[b]
        out_ref[...] = final_math(total, *[ref[...] for ref in refs])

    return call(kernel, plain(ROWS, SHARE), (), arrays)


def swap(values, axis):
    return lax.all_to_all(values, axis, 0, 0, tiled=True)


def local(mask_param, target, source_weight, row_shift, col_shift):
    half, at, core = (lax.axis_index(name) for name in ("zh", "x", "c"))
    src_index = lax.axis_index(("zh", "x", "c"))
    row_index = lax.axis_index(("zl", "y"))
    places = [at, at ^ 1, 3 - at, (3 - at) ^ 1]
    shares = jnp.stack([2 * place + side for place in places for side in (core, 1 - core)])
    shifts = half * (MC // 2) + STEP * shares
    other = lax.ppermute(target, "c", [(0, 1), (1, 0)])
    sent, turn = columns_part(row_index, mask_param)
    two = jnp.stack([target, other])
    second = lax.ppermute(two, "x", [(i, i ^ 1) for i in range(4)])
    heard = swap(sent, ("zl", "y"))
    four = jnp.concatenate([two, second])
    third = lax.ppermute(four, "x", [(i, 3 - i) for i in range(4)])
    targets = (two, second, third)
    message = middle_part(shifts, source_weight, row_shift, col_shift, heard, targets, turn)
    message = repeat_sum(swap(message, "y"))
    return final_part(src_index, row_index, swap(message, ("zh", "zl")), mask_param)


def solution(mesh):
    fine = Mesh(mesh.devices.reshape(2, 4, 2, 4, 8), ("zh", "x", "c", "zl", "y"))
    rows, src = ("zl", "y"), ("zh", "x", "c")
    placed = (P(rows, None), P(rows, src), P(), P(), P())
    return jax.shard_map(
        local, mesh=fine, in_specs=placed, out_specs=P(rows, src), check_vma=False
    )
```

profile of v0, /device:TPU:6, one launch (start us, length us, event | category | flops | bytes accessed | tf_op | source)
XLA Modules:
  0.0 73.4 jit_solution(1484472299061459540)
XLA Ops:
  0.0 1.9 %collective-permute-start = (s32[16,512]{1,0:T(8,128)}, s32[16,512]{1,0:T(8,128)S(1)}, u32[]{:S(2)}, u32[]{:S(2)}) collective-permute-start(s32[16,512]{1,0:T(8,128)} %param.25), channel_id=1, source_target_pairs={{0,32},{32,0},{1,33},{33,1},{2,34},{34,2},{3,35},{35,3},{4,36},{36... | collective-permute-start | bytes 98312 | tf_op jit(solution)/shard_map/ppermute | solution.py:464
  1.9 0.0 copy-start.11
  1.9 0.0 copy-start.1
  1.9 0.0 copy-start.8
  2.0 2.7 %columns_part.1 = (f32[544,128]{1,0:T(8,128)}, f32[32,64]{1,0:T(8,128)S(1)}) custom-call(s32[1]{0:T(128)} %bitcast.8.place, f32[16,8192]{1,0:T(8,128)} %mask_ref.1, f32[32,32,64]{2,1,0:T(8,128)} %constant.87.clone.turn_ref, f32[136,512]{1,0:T(8,128)} %constant.88.clone.refs_0_, f32[16,128]{1,0:T(8,128)} %constant.89.clone.refs_1_, ...), custom_call_target="tpu_custom_call" | custom-call | tf_op jit(solution)/shard_map/columns_part/pallas_call | solution.py:357
  4.7 0.0 copy-start
  4.7 0.0 copy-start.7
  4.7 13.0 %all-to-all-start = ((f32[32,1,2176]{2,1,0:T(1,128)}), f32[32,1,2176]{2,1,0:T(1,128)S(1)}, u32[]{:S(2)}, u32[]{:S(2)}) async-start(f32[32,1,2176]{2,1,0:T(1,128)} %bitcast.9), calls=%async_computation | async-start | bytes 557056 | tf_op jit(solution)/shard_map/all_to_all | solution.py:454
  17.8 0.0 collective-permute-done
  17.8 0.0 copy-done.11
  17.8 0.0 copy-start.5
  17.8 0.0 copy-start.9
  17.8 2.9 %collective-permute-start.1 = (s32[2,16,512]{2,1,0:T(8,128)S(1)}, s32[2,16,512]{2,1,0:T(8,128)S(1)}, u32[]{:S(2)}, u32[]{:S(2)}) collective-permute-start(s32[2,16,512]{2,1,0:T(8,128)S(1)} %pad_add_fusion.1), channel_id=1, source_target_pairs={{0,64},{64,0},{128,192},{192,128},{1,65},{65,1},{129,193},{193,129... | collective-permute-start | bytes 196616 | tf_op jit(solution)/shard_map/ppermute | solution.py:467
  20.7 0.0 copy-start.6
  20.7 0.1 stack.44
  20.8 0.0 copy-start.3
  20.8 0.0 copy-start.4
  20.8 3.3 %collective-permute-done.1 = s32[2,16,512]{2,1,0:T(8,128)S(1)} collective-permute-done((s32[2,16,512]{2,1,0:T(8,128)S(1)}, s32[2,16,512]{2,1,0:T(8,128)S(1)}, u32[]{:S(2)}, u32[]{:S(2)}) %collective-permute-start.1) | collective-permute-done | bytes 65568 | tf_op jit(solution)/shard_map/ppermute | solution.py:467
  24.1 2.4 %collective-permute-start.2 = (s32[4,16,512]{2,1,0:T(8,128)S(1)}, s32[4,16,512]{2,1,0:T(8,128)S(1)}, u32[]{:S(2)}, u32[]{:S(2)}) collective-permute-start(s32[4,16,512]{2,1,0:T(8,128)S(1)} %pad_add_fusion), channel_id=1, source_target_pairs={{0,192},{64,128},{128,64},{192,0},{1,193},{65,129},{129,65},{193,1... | collective-permute-start | bytes 393224 | tf_op jit(solution)/shard_map/ppermute | solution.py:470
  26.5 0.6 multiply_add_fusion.shift_ref
  27.1 5.1 %collective-permute-done.2 = s32[4,16,512]{2,1,0:T(8,128)S(1)} collective-permute-done((s32[4,16,512]{2,1,0:T(8,128)S(1)}, s32[4,16,512]{2,1,0:T(8,128)S(1)}, u32[]{:S(2)}, u32[]{:S(2)}) %collective-permute-start.2) | collective-permute-done | bytes 131104 | tf_op jit(solution)/shard_map/ppermute | solution.py:470
  32.2 0.0 all-to-all-done
  32.2 0.0 copy-done.1
  32.2 0.0 copy-done.8
  32.2 0.0 copy-done
  32.2 0.0 copy-done.7
  32.2 0.0 copy-done.5
  32.2 0.0 copy-done.9
  32.2 0.0 copy-done.6
  32.3 0.0 copy-done.3
  32.3 0.0 copy-done.4
  32.3 5.7 %shard_map.226 = f32[8,40,128]{2,1,0:T(8,128)} custom-call(s32[8]{0:T(128)} %multiply_add_fusion.shift_ref, f32[16]{0:T(128)} %weight_ref.1, s32[16]{0:T(128)} %row_ref.1, s32[16]{0:T(128)} %col_ref.1, f32[544,128]{1,0:T(8,128)S(1)} %bitcast.22, s32[32,512]{1,0:T(8,128)S(1)} %bitcast.23, s32[32,512]{1,0:T(8,128)S(1)} %bitcast.24, s32[64,512]{1,0:T(8,128)S(1)} %bitcast.25, ...), custom_call_target="tpu_custom_call" | custom-call | tf_op jit(solution)/shard_map/pallas_call | solution.py:321
  38.0 7.0 %all-to-all-start.1 = ((f32[8,40,128]{2,1,0:T(8,128)}), f32[8,40,128]{2,1,0:T(8,128)S(1)}, u32[]{:S(2)}, u32[]{:S(2)}) async-start(f32[8,40,128]{2,1,0:T(8,128)} %shard_map.226), calls=%async_computation.1 | async-start | bytes 327680 | tf_op jit(solution)/shard_map/all_to_all | solution.py:454
  44.9 9.4 %all-to-all-done.1.in_ref = f32[8,40,128]{2,1,0:T(8,128)S(1)} async-done(((f32[8,40,128]{2,1,0:T(8,128)}), f32[8,40,128]{2,1,0:T(8,128)S(1)}, u32[]{:S(2)}, u32[]{:S(2)}) %all-to-all-start.1) | async-done | bytes 163872 | tf_op jit(solution)/shard_map/all_to_all | solution.py:454
  54.4 0.7 shard_map.227
  55.1 0.0 copy-start.2
  55.1 7.8 %all-to-all-start.2 = ((f32[8,40,128]{2,1,0:T(8,128)}), f32[8,40,128]{2,1,0:T(8,128)S(1)}, u32[]{:S(2)}, u32[]{:S(2)}) async-start(f32[8,40,128]{2,1,0:T(8,128)} %shard_map.227), calls=%async_computation.2 | async-start | bytes 327680 | tf_op jit(solution)/shard_map/all_to_all | solution.py:454
  62.9 0.7 fusion
  63.5 0.7 dynamic-slice_bitcast_fusion.refs_1_
  64.2 0.8 %constant_dynamic-slice_fusion.2.refs_0_ = f32[16,512]{1,0:T(8,128)S(1)} fusion(f32[16,8192]{1,0:T(8,128)} %mask_ref.1, s32[]{:T(128)S(6)} %select_n.12), kind=kLoop, calls=%fused_computation.5 | loop fusion | bytes 65540 | tf_op jit(solution)/shard_map/dynamic_slice | solution.py:434
  65.0 0.0 copy-start.10
  65.0 7.3 %all-to-all-done.2.in_ref = f32[8,40,128]{2,1,0:T(8,128)S(1)} async-done(((f32[8,40,128]{2,1,0:T(8,128)}), f32[8,40,128]{2,1,0:T(8,128)S(1)}, u32[]{:S(2)}, u32[]{:S(2)}) %all-to-all-start.2) | async-done | bytes 163872 | tf_op jit(solution)/shard_map/all_to_all | solution.py:454
  72.3 0.0 copy-done.2
  72.3 0.0 copy-done.10
  72.3 1.1 %shard_map.228 = f32[16,512]{1,0:T(8,128)} custom-call(f32[8,40,128]{2,1,0:T(8,128)S(1)} %all-to-all-done.2.in_ref, f32[16,512]{1,0:T(8,128)S(1)} %constant_dynamic-slice_fusion.2.refs_0_, f32[16,128]{1,0:T(8,128)S(1)} %dynamic-slice_bitcast_fusion.refs_1_, f32[1,128]{1,0:T(1,128)S(1)} %get-tuple-element.9.refs_2_, f32[1,128]{1,0:T(1,128)S(1)} %get-tuple-element.10.refs_3_, ...), custom_call_target="tpu_custom_call" | custom-call | tf_op jit(solution)/shard_map/pallas_call | solution.py:321
  (2 shorter events, 0.0 us)
Async XLA Ops:
  0.0 17.8 %collective-permute-start = (s32[16,512]{1,0:T(8,128)}, s32[16,512]{1,0:T(8,128)S(1)}, u32[]{:S(2)}, u32[]{:S(2)}) collective-permute-start(s32[16,512]{1,0:T(8,128)} %param.25), channel_id=1, source_target_pairs={{0,32},{32,0},{1,33},{33,1},{2,34},{34,2},{3,35},{35,3},{4,36},{36... | collective-permute-start | bytes 98312 | tf_op jit(solution)/shard_map/ppermute | solution.py:464
  1.9 15.8 %copy-start.11 = (s32[16,512]{1,0:T(8,128)S(1)}, s32[16,512]{1,0:T(8,128)}, u32[]{:S(2)}) copy-start(s32[16,512]{1,0:T(8,128)} %param.25) | copy-start | bytes 98308
  1.9 30.3 %copy-start.1 = (f32[256,512]{1,0:T(8,128)S(1)}, f32[256,512]{1,0:T(8,128)}, u32[]{:S(2)}) copy-start(f32[256,512]{1,0:T(8,128)} %constant.97.clone.refs_9_) | copy-start | bytes 1572868
  1.9 30.3 %copy-start.8 = (f32[64,32]{1,0:T(8,128)S(1)}, f32[64,32]{1,0:T(8,128)}, u32[]{:S(2)}) copy-start(f32[64,32]{1,0:T(8,128)} %constant.94.clone.refs_6_) | copy-start | bytes 24580
  4.7 27.5 %copy-start = (f32[256,512]{1,0:T(8,128)S(1)}, f32[256,512]{1,0:T(8,128)}, u32[]{:S(2)}) copy-start(f32[256,512]{1,0:T(8,128)} %constant.96.clone.refs_8_) | copy-start | bytes 1572868
  4.7 27.5 %copy-start.7 = (f32[64,128]{1,0:T(8,128)S(1)}, f32[64,128]{1,0:T(8,128)}, u32[]{:S(2)}) copy-start(f32[64,128]{1,0:T(8,128)} %constant.93.clone.refs_5_) | copy-start | bytes 98308
  4.7 27.5 %all-to-all-start = ((f32[32,1,2176]{2,1,0:T(1,128)}), f32[32,1,2176]{2,1,0:T(1,128)S(1)}, u32[]{:S(2)}, u32[]{:S(2)}) async-start(f32[32,1,2176]{2,1,0:T(1,128)} %bitcast.9), calls=%async_computation | async-start | bytes 557056 | tf_op jit(solution)/shard_map/all_to_all | solution.py:454
  17.8 14.5 %copy-start.5 = (f32[128,256]{1,0:T(8,128)S(1)}, f32[128,256]{1,0:T(8,128)}, u32[]{:S(2)}) copy-start(f32[128,256]{1,0:T(8,128)} %constant.98.clone.refs_10_) | copy-start | bytes 393220
  17.8 14.4 %copy-start.9 = (f32[8,128]{1,0:T(8,128)S(1)}, f32[8,128]{1,0:T(8,128)}, u32[]{:S(2)}) copy-start(f32[8,128]{1,0:T(8,128)} %constant.91.clone.refs_3_.refs_12_) | copy-start | bytes 12292
  17.8 6.3 %collective-permute-start.1 = (s32[2,16,512]{2,1,0:T(8,128)S(1)}, s32[2,16,512]{2,1,0:T(8,128)S(1)}, u32[]{:S(2)}, u32[]{:S(2)}) collective-permute-start(s32[2,16,512]{2,1,0:T(8,128)S(1)} %pad_add_fusion.1), channel_id=1, source_target_pairs={{0,64},{64,0},{128,192},{192,128},{1,65},{65,1},{129,193},{193,129... | collective-permute-start | bytes 196616 | tf_op jit(solution)/shard_map/ppermute | solution.py:467
  20.7 11.5 %copy-start.6 = (f32[128,64]{1,0:T(8,128)S(1)}, f32[128,64]{1,0:T(8,128)}, u32[]{:S(2)}) copy-start(f32[128,64]{1,0:T(8,128)} %constant.99.clone.refs_11_) | copy-start | bytes 98308
  20.8 11.4 %copy-start.3 = (f32[64,512]{1,0:T(8,128)S(1)}, f32[64,512]{1,0:T(8,128)}, u32[]{:S(2)}) copy-start(f32[64,512]{1,0:T(8,128)} %constant.92.clone.refs_4_) | copy-start | bytes 393220
  20.8 11.5 %copy-start.4 = (f32[128,256]{1,0:T(8,128)S(1)}, f32[128,256]{1,0:T(8,128)}, u32[]{:S(2)}) copy-start(f32[128,256]{1,0:T(8,128)} %constant.95.clone.refs_7_) | copy-start | bytes 393220
  24.1 8.1 %collective-permute-start.2 = (s32[4,16,512]{2,1,0:T(8,128)S(1)}, s32[4,16,512]{2,1,0:T(8,128)S(1)}, u32[]{:S(2)}, u32[]{:S(2)}) collective-permute-start(s32[4,16,512]{2,1,0:T(8,128)S(1)} %pad_add_fusion), channel_id=1, source_target_pairs={{0,192},{64,128},{128,64},{192,0},{1,193},{65,129},{129,65},{193,1... | collective-permute-start | bytes 393224 | tf_op jit(solution)/shard_map/ppermute | solution.py:470
  38.0 16.4 %all-to-all-start.1 = ((f32[8,40,128]{2,1,0:T(8,128)}), f32[8,40,128]{2,1,0:T(8,128)S(1)}, u32[]{:S(2)}, u32[]{:S(2)}) async-start(f32[8,40,128]{2,1,0:T(8,128)} %shard_map.226), calls=%async_computation.1 | async-start | bytes 327680 | tf_op jit(solution)/shard_map/all_to_all | solution.py:454
  55.1 17.2 %copy-start.2 = (f32[128,512]{1,0:T(8,128)S(1)}, f32[128,512]{1,0:T(8,128)}, u32[]{:S(2)}) copy-start(f32[128,512]{1,0:T(8,128)} %constant.103.clone.refs_4_) | copy-start | bytes 786436
  55.1 17.2 %all-to-all-start.2 = ((f32[8,40,128]{2,1,0:T(8,128)}), f32[8,40,128]{2,1,0:T(8,128)S(1)}, u32[]{:S(2)}, u32[]{:S(2)}) async-start(f32[8,40,128]{2,1,0:T(8,128)} %shard_map.227), calls=%async_computation.2 | async-start | bytes 327680 | tf_op jit(solution)/shard_map/all_to_all | solution.py:454
  65.0 7.3 %copy-start.10 = (f32[1,512]{1,0:T(1,128)S(1)}, f32[1,512]{1,0:T(1,128)}, u32[]{:S(2)}) copy-start(f32[1,512]{1,0:T(1,128)} %constant.104.clone.refs_5_) | copy-start | bytes 6148
where the time goes:
time: 74 us; the launch traced here: 73.4 us
  starting transfers between devices  35 us (47%)
  waiting for transfers between devices  25.1 us (34%)
  Pallas kernels  10.2 us (14%)
  local copies, waits for them, and re-layouts  2.28 us (3%)
    all_to_all x3, starting transfers between devices, swap(): return lax.all_to_all(values, axis, 0, 0, tiled=True)  27.8 us
    all_to_all x3, waiting for transfers between devices, swap(): return lax.all_to_all(values, axis, 0, 0, tiled=True)  16.7 us
    pallas_call x3, Pallas kernels, call(): pl.pallas_call(body, in_specs=[SMEM] * len(scalars) + [VMEM] * len(arrays...  7.44 us
    ppermute x1, waiting for transfers between devices, local(): third = lax.ppermute(four, 'x', [(i, 3 - i) for i in range(4)])  5.1 us
    ppermute x1, waiting for transfers between devices, local(): second = lax.ppermute(two, 'x', [(i, i ^ 1) for i in range(4)])  3.29 us
    ppermute x1, starting transfers between devices, local(): second = lax.ppermute(two, 'x', [(i, i ^ 1) for i in range(4)])  2.87 us
    pallas_call x1, Pallas kernels, columns_part(): pl.pallas_call(kernel, grid_spec=pltpu.PrefetchScalarGridSpec(num_scalar_...  2.74 us
    ppermute x1, starting transfers between devices, local(): third = lax.ppermute(four, 'x', [(i, 3 - i) for i in range(4)])  2.39 us
  transfers between devices with their start and end apart: 6, of which 4 were waited for; matrix products, arithmetic and copies ran while one was open for 4% of the time, Pallas kernels for 4%

commit v1 on v0

--- a/solution.py
+++ b/solution.py
@@ -30,6 +30,9 @@
 NEAR = 8
 STEP = MC // BLOCKS
 LINES = ROWS + 1
+ROW_ORDER = None
+Y_ORDER = [4, 5, 6, 7, 0, 1, 2, 3]
+Z_ORDER = [4, 5, 6, 7, 0, 1, 2, 3]
 UNIT = 1.0 / math.sqrt(NR * NC)
 
 
@@ -151,10 +154,30 @@
     return one(high, right_high) + (one(high, right_low) + one(low, right_high))
 
 
-def dot_tn(left, right):
-    return lax.dot_general(
-        left, right, (((0,), (0,)), ((), ())), precision=highest, preferred_element_type=jnp.float32
-    )
+def dot3_tn(left, right):
+    left_high, left_low = split(left)
+    right_high, right_low = split(right)
+    one = lambda a, b: lax.dot_general(
+        a, b, (((0,), (0,)), ((), ())), preferred_element_type=jnp.float32
+    )
+    return one(left_high, right_high) + (one(left_high, right_low) + one(left_low, right_high))
+
+
+def dot_signs(left, right, signs_left):
+    one = lambda a, b: jnp.dot(a, b, preferred_element_type=jnp.float32)
+    values, signs = (right, left) if signs_left else (left, right)
+    signs = signs.astype(jnp.bfloat16)
+    total = None
+    for part in split3(values):
+        now = one(signs, part) if signs_left else one(part, signs)
+        total = now if total is None else total + now
+    return total
+
+
+def split3(values):
+    high, low = split(values)
+    rest = values - high.astype(jnp.float32) - low.astype(jnp.float32)
+    return high, low, rest.astype(jnp.bfloat16)
 
 
 def logistic(values):
@@ -216,7 +239,7 @@
     fold_rows,
     pick,
 ):
-    both = dot(dot(rows, main), spread)
+    both = dot_signs(dot(rows, main), spread, False)
     inside = dot_nt(inner, edge)
     in_cos, in_sin = inside[:KR], inside[KR:]
     out_cos, out_sin = outer[:KR], outer[KR:]
@@ -287,18 +310,20 @@
         ],
         axis=1,
     )
-    spectra = dot_tn(turn, back)
+    spectra = dot3_tn(turn, back)
     adjoint_real = jnp.zeros((KR, KC), jnp.float32)
     adjoint_imag = jnp.zeros((KR, KC), jnp.float32)
     for s in range(POINTS):
         now = spectra[:, KC * s : KC * (s + 1)]
         adjoint_real = adjoint_real + opened[s] * now[:KR]
         adjoint_imag = adjoint_imag + opened[s] * now[KR:]
-    folded = dot(jnp.concatenate([adjoint_real, adjoint_imag], axis=0), fold_columns)
+    folded = dot_signs(
+        jnp.concatenate([adjoint_real, adjoint_imag], axis=0), fold_columns, False
+    )
     real, imag = folded[:KR], folded[KR:]
     even = lanes((KR, 2 * KC)) <= HALF
     kinds = jnp.concatenate([jnp.where(even, real, imag), jnp.where(even, -imag, real)], axis=0)
-    packed = dot(fold_rows, kinds)
+    packed = dot_signs(fold_rows, kinds, True)
     last = dot_nt(pick, packed[:, KC:])
     return jnp.concatenate([packed[:KR, :KC], packed[KR : KR + 8, :KC] + last], axis=0)
 
@@ -450,8 +475,9 @@
     return call(kernel, plain(ROWS, SHARE), (), arrays)
 
 
-def swap(values, axis):
-    return lax.all_to_all(values, axis, 0, 0, tiled=True)
+def swap(values, axis, order=None):
+    groups = None if order is None else [order]
+    return lax.all_to_all(values, axis, 0, 0, axis_index_groups=groups, tiled=True)
 
 
 def local(mask_param, target, source_weight, row_shift, col_shift):
@@ -465,13 +491,13 @@
     sent, turn = columns_part(row_index, mask_param)
     two = jnp.stack([target, other])
     second = lax.ppermute(two, "x", [(i, i ^ 1) for i in range(4)])
-    heard = swap(sent, ("zl", "y"))
+    heard = swap(sent, ("zl", "y"), ROW_ORDER)
     four = jnp.concatenate([two, second])
     third = lax.ppermute(four, "x", [(i, 3 - i) for i in range(4)])
     targets = (two, second, third)
     message = middle_part(shifts, source_weight, row_shift, col_shift, heard, targets, turn)
-    message = repeat_sum(swap(message, "y"))
-    return final_part(src_index, row_index, swap(message, ("zh", "zl")), mask_param)
+    message = repeat_sum(swap(message, "y", Y_ORDER))
+    return final_part(src_index, row_index, swap(message, ("zh", "zl"), Z_ORDER), mask_param)
 
 
 def solution(mesh):

time: 74 us -> 68.2 us (0.922)
  waiting for transfers between devices: 25.1 us -> 14.4 us
  starting transfers between devices: 35 us -> 40.3 us
    all_to_all x3, waiting for transfers between devices: 16.7 us -> 5.97 us  [swap(): lax.all_to_all(values, axis, 0, 0, axis_index_groups=groups, tiled=True)]
    all_to_all x3, starting transfers between devices: 27.8 us -> 33.1 us  [swap(): lax.all_to_all(values, axis, 0, 0, axis_index_groups=groups, tiled=True)]
where the time goes in v1:
time: 68.2 us; the launch traced here: 67.6 us
  starting transfers between devices  40.3 us (59%)
  waiting for transfers between devices  14.4 us (21%)
  Pallas kernels  9.88 us (14%)
  local copies, waits for them, and re-layouts  2.28 us (3%)
    all_to_all x3, starting transfers between devices, swap(): lax.all_to_all(values, axis, 0, 0, axis_index_groups=groups, tiled=True)  33.1 us
    pallas_call x3, Pallas kernels, call(): pl.pallas_call(body, in_specs=[SMEM] * len(scalars) + [VMEM] * len(arrays...  7.14 us
    all_to_all x3, waiting for transfers between devices, swap(): lax.all_to_all(values, axis, 0, 0, axis_index_groups=groups, tiled=True)  5.97 us
    ppermute x1, waiting for transfers between devices, local(): third = lax.ppermute(four, 'x', [(i, 3 - i) for i in range(4)])  5.1 us
    ppermute x1, waiting for transfers between devices, local(): second = lax.ppermute(two, 'x', [(i, i ^ 1) for i in range(4)])  3.29 us
    ppermute x1, starting transfers between devices, local(): second = lax.ppermute(two, 'x', [(i, i ^ 1) for i in range(4)])  2.87 us
    pallas_call x1, Pallas kernels, columns_part(): pl.pallas_call(kernel, grid_spec=pltpu.PrefetchScalarGridSpec(num_scalar_...  2.74 us
    ppermute x1, starting transfers between devices, local(): third = lax.ppermute(four, 'x', [(i, 3 - i) for i in range(4)])  2.39 us
  transfers between devices with their start and end apart: 6, of which 4 were waited for; matrix products, arithmetic and copies ran while one was open for 4% of the time, Pallas kernels for 4%

profile of v1, /device:TPU:6, one launch (start us, length us, event | category | flops | bytes accessed | tf_op | source)
XLA Modules:
  0.0 67.6 jit_solution(16609656978516373926)
XLA Ops:
  0.0 1.9 %collective-permute-start = (s32[16,512]{1,0:T(8,128)}, s32[16,512]{1,0:T(8,128)S(1)}, u32[]{:S(2)}, u32[]{:S(2)}) collective-permute-start(s32[16,512]{1,0:T(8,128)} %param.25), channel_id=1, source_target_pairs={{0,32},{32,0},{1,33},{33,1},{2,34},{34,2},{3,35},{35,3},{4,36},{36... | collective-permute-start | bytes 98312 | tf_op jit(solution)/shard_map/ppermute | solution.py:490
  1.9 0.0 copy-start.11
  1.9 0.0 copy-start.1
  1.9 0.0 copy-start.8
  2.0 2.7 %columns_part.1 = (f32[544,128]{1,0:T(8,128)}, f32[32,64]{1,0:T(8,128)S(1)}) custom-call(s32[1]{0:T(128)} %bitcast.8.place, f32[16,8192]{1,0:T(8,128)} %mask_ref.1, f32[32,32,64]{2,1,0:T(8,128)} %constant.87.clone.turn_ref, f32[136,512]{1,0:T(8,128)} %constant.88.clone.refs_0_, f32[16,128]{1,0:T(8,128)} %constant.89.clone.refs_1_, ...), custom_call_target="tpu_custom_call" | custom-call | tf_op jit(solution)/shard_map/columns_part/pallas_call | solution.py:382
  4.7 0.0 copy-start
  4.7 0.0 copy-start.7
  4.7 13.0 %all-to-all-start = ((f32[32,1,2176]{2,1,0:T(1,128)}), f32[32,1,2176]{2,1,0:T(1,128)S(1)}, u32[]{:S(2)}, u32[]{:S(2)}) async-start(f32[32,1,2176]{2,1,0:T(1,128)} %bitcast.9), calls=%async_computation | async-start | bytes 557056 | tf_op jit(solution)/shard_map/all_to_all | solution.py:480
  17.8 0.0 collective-permute-done
  17.8 0.0 copy-done.11
  17.8 0.0 copy-start.5
  17.8 0.0 copy-start.9
  17.8 2.9 %collective-permute-start.1 = (s32[2,16,512]{2,1,0:T(8,128)S(1)}, s32[2,16,512]{2,1,0:T(8,128)S(1)}, u32[]{:S(2)}, u32[]{:S(2)}) collective-permute-start(s32[2,16,512]{2,1,0:T(8,128)S(1)} %pad_add_fusion.1), channel_id=1, source_target_pairs={{0,64},{64,0},{128,192},{192,128},{1,65},{65,1},{129,193},{193,129... | collective-permute-start | bytes 196616 | tf_op jit(solution)/shard_map/ppermute | solution.py:493
  20.7 0.0 copy-start.6
  20.7 0.1 stack.44
  20.8 0.0 copy-start.3
  20.8 0.0 copy-start.4
  20.8 3.3 %collective-permute-done.1 = s32[2,16,512]{2,1,0:T(8,128)S(1)} collective-permute-done((s32[2,16,512]{2,1,0:T(8,128)S(1)}, s32[2,16,512]{2,1,0:T(8,128)S(1)}, u32[]{:S(2)}, u32[]{:S(2)}) %collective-permute-start.1) | collective-permute-done | bytes 65568 | tf_op jit(solution)/shard_map/ppermute | solution.py:493
  24.1 2.4 %collective-permute-start.2 = (s32[4,16,512]{2,1,0:T(8,128)S(1)}, s32[4,16,512]{2,1,0:T(8,128)S(1)}, u32[]{:S(2)}, u32[]{:S(2)}) collective-permute-start(s32[4,16,512]{2,1,0:T(8,128)S(1)} %pad_add_fusion), channel_id=1, source_target_pairs={{0,192},{64,128},{128,64},{192,0},{1,193},{65,129},{129,65},{193,1... | collective-permute-start | bytes 393224 | tf_op jit(solution)/shard_map/ppermute | solution.py:496
  26.5 0.6 multiply_add_fusion.shift_ref
  27.1 5.1 %collective-permute-done.2 = s32[4,16,512]{2,1,0:T(8,128)S(1)} collective-permute-done((s32[4,16,512]{2,1,0:T(8,128)S(1)}, s32[4,16,512]{2,1,0:T(8,128)S(1)}, u32[]{:S(2)}, u32[]{:S(2)}) %collective-permute-start.2) | collective-permute-done | bytes 131104 | tf_op jit(solution)/shard_map/ppermute | solution.py:496
  32.2 0.0 all-to-all-done
  32.2 0.0 copy-done.1
  32.2 0.0 copy-done.8
  32.2 0.0 copy-done
  32.2 0.0 copy-done.7
  32.2 0.0 copy-done.5
  32.2 0.0 copy-done.9
  32.2 0.0 copy-done.6
  32.3 0.0 copy-done.3
  32.3 0.0 copy-done.4
  32.3 5.4 %shard_map.226 = f32[8,40,128]{2,1,0:T(8,128)} custom-call(s32[8]{0:T(128)} %multiply_add_fusion.shift_ref, f32[16]{0:T(128)} %weight_ref.1, s32[16]{0:T(128)} %row_ref.1, s32[16]{0:T(128)} %col_ref.1, f32[544,128]{1,0:T(8,128)S(1)} %bitcast.22, s32[32,512]{1,0:T(8,128)S(1)} %bitcast.23, s32[32,512]{1,0:T(8,128)S(1)} %bitcast.24, s32[64,512]{1,0:T(8,128)S(1)} %bitcast.25, ...), custom_call_target="tpu_custom_call" | custom-call | tf_op jit(solution)/shard_map/pallas_call | solution.py:346
  37.7 9.0 %all-to-all-start.1 = ((f32[8,40,128]{2,1,0:T(8,128)}), f32[8,40,128]{2,1,0:T(8,128)S(1)}, u32[]{:S(2)}, u32[]{:S(2)}) async-start(f32[8,40,128]{2,1,0:T(8,128)} %shard_map.226), calls=%async_computation.1 | async-start | bytes 327680 | tf_op jit(solution)/shard_map/all_to_all | solution.py:480
  46.7 4.0 %all-to-all-done.1.in_ref = f32[8,40,128]{2,1,0:T(8,128)S(1)} async-done(((f32[8,40,128]{2,1,0:T(8,128)}), f32[8,40,128]{2,1,0:T(8,128)S(1)}, u32[]{:S(2)}, u32[]{:S(2)}) %all-to-all-start.1) | async-done | bytes 163872 | tf_op jit(solution)/shard_map/all_to_all | solution.py:480
  50.7 0.7 %shard_map.227 = f32[8,40,128]{2,1,0:T(8,128)} custom-call(f32[8,40,128]{2,1,0:T(8,128)S(1)} %all-to-all-done.1.in_ref), custom_call_target="tpu_custom_call" | custom-call | tf_op jit(solution)/shard_map/pallas_call | solution.py:346
  51.4 0.0 copy-start.2
  51.4 11.0 %all-to-all-start.2 = ((f32[8,40,128]{2,1,0:T(8,128)}), f32[8,40,128]{2,1,0:T(8,128)S(1)}, u32[]{:S(2)}, u32[]{:S(2)}) async-start(f32[8,40,128]{2,1,0:T(8,128)} %shard_map.227), calls=%async_computation.2 | async-start | bytes 327680 | tf_op jit(solution)/shard_map/all_to_all | solution.py:480
  62.4 0.7 fusion
  63.1 0.7 %dynamic-slice_bitcast_fusion.refs_1_ = f32[16,128]{1,0:T(8,128)S(1)} fusion(f32[32,16,128]{2,1,0:T(8,128)} %constant.100.clone, s32[]{:T(128)S(6)} %select_n.13), kind=kLoop, calls=%fused_computation.2 | loop fusion | bytes 16388 | tf_op jit(solution)/shard_map/jit(dynamic_index_in_dim)/squeeze | solution.py:359
  63.8 0.8 %constant_dynamic-slice_fusion.2.refs_0_ = f32[16,512]{1,0:T(8,128)S(1)} fusion(f32[16,8192]{1,0:T(8,128)} %mask_ref.1, s32[]{:T(128)S(6)} %select_n.12), kind=kLoop, calls=%fused_computation.5 | loop fusion | bytes 65540 | tf_op jit(solution)/shard_map/dynamic_slice | solution.py:459
  64.6 0.0 copy-start.10
  64.6 1.9 %all-to-all-done.2.in_ref = f32[8,40,128]{2,1,0:T(8,128)S(1)} async-done(((f32[8,40,128]{2,1,0:T(8,128)}), f32[8,40,128]{2,1,0:T(8,128)S(1)}, u32[]{:S(2)}, u32[]{:S(2)}) %all-to-all-start.2) | async-done | bytes 163872 | tf_op jit(solution)/shard_map/all_to_all | solution.py:480
  66.5 0.0 copy-done.2
  66.5 0.0 copy-done.10
  66.5 1.1 %shard_map.228 = f32[16,512]{1,0:T(8,128)} custom-call(f32[8,40,128]{2,1,0:T(8,128)S(1)} %all-to-all-done.2.in_ref, f32[16,512]{1,0:T(8,128)S(1)} %constant_dynamic-slice_fusion.2.refs_0_, f32[16,128]{1,0:T(8,128)S(1)} %dynamic-slice_bitcast_fusion.refs_1_, f32[1,128]{1,0:T(1,128)S(1)} %get-tuple-element.9.refs_2_, f32[1,128]{1,0:T(1,128)S(1)} %get-tuple-element.10.refs_3_, ...), custom_call_target="tpu_custom_call" | custom-call | tf_op jit(solution)/shard_map/pallas_call | solution.py:346
  (2 shorter events, 0.0 us)
Async XLA Ops:
  0.0 17.8 %collective-permute-start = (s32[16,512]{1,0:T(8,128)}, s32[16,512]{1,0:T(8,128)S(1)}, u32[]{:S(2)}, u32[]{:S(2)}) collective-permute-start(s32[16,512]{1,0:T(8,128)} %param.25), channel_id=1, source_target_pairs={{0,32},{32,0},{1,33},{33,1},{2,34},{34,2},{3,35},{35,3},{4,36},{36... | collective-permute-start | bytes 98312 | tf_op jit(solution)/shard_map/ppermute | solution.py:490
  1.9 15.8 %copy-start.11 = (s32[16,512]{1,0:T(8,128)S(1)}, s32[16,512]{1,0:T(8,128)}, u32[]{:S(2)}) copy-start(s32[16,512]{1,0:T(8,128)} %param.25) | copy-start | bytes 98308
  1.9 30.3 %copy-start.1 = (f32[256,512]{1,0:T(8,128)S(1)}, f32[256,512]{1,0:T(8,128)}, u32[]{:S(2)}) copy-start(f32[256,512]{1,0:T(8,128)} %constant.97.clone.refs_9_) | copy-start | bytes 1572868
  1.9 30.3 %copy-start.8 = (f32[64,32]{1,0:T(8,128)S(1)}, f32[64,32]{1,0:T(8,128)}, u32[]{:S(2)}) copy-start(f32[64,32]{1,0:T(8,128)} %constant.94.clone.refs_6_) | copy-start | bytes 24580
  4.7 27.5 %copy-start = (f32[256,512]{1,0:T(8,128)S(1)}, f32[256,512]{1,0:T(8,128)}, u32[]{:S(2)}) copy-start(f32[256,512]{1,0:T(8,128)} %constant.96.clone.refs_8_) | copy-start | bytes 1572868
  4.7 27.5 %copy-start.7 = (f32[64,128]{1,0:T(8,128)S(1)}, f32[64,128]{1,0:T(8,128)}, u32[]{:S(2)}) copy-start(f32[64,128]{1,0:T(8,128)} %constant.93.clone.refs_5_) | copy-start | bytes 98308
  4.7 27.5 %all-to-all-start = ((f32[32,1,2176]{2,1,0:T(1,128)}), f32[32,1,2176]{2,1,0:T(1,128)S(1)}, u32[]{:S(2)}, u32[]{:S(2)}) async-start(f32[32,1,2176]{2,1,0:T(1,128)} %bitcast.9), calls=%async_computation | async-start | bytes 557056 | tf_op jit(solution)/shard_map/all_to_all | solution.py:480
  17.8 14.5 %copy-start.5 = (f32[128,256]{1,0:T(8,128)S(1)}, f32[128,256]{1,0:T(8,128)}, u32[]{:S(2)}) copy-start(f32[128,256]{1,0:T(8,128)} %constant.98.clone.refs_10_) | copy-start | bytes 393220
  17.8 14.4 %copy-start.9 = (f32[8,128]{1,0:T(8,128)S(1)}, f32[8,128]{1,0:T(8,128)}, u32[]{:S(2)}) copy-start(f32[8,128]{1,0:T(8,128)} %constant.91.clone.refs_3_.refs_12_) | copy-start | bytes 12292
  17.8 6.3 %collective-permute-start.1 = (s32[2,16,512]{2,1,0:T(8,128)S(1)}, s32[2,16,512]{2,1,0:T(8,128)S(1)}, u32[]{:S(2)}, u32[]{:S(2)}) collective-permute-start(s32[2,16,512]{2,1,0:T(8,128)S(1)} %pad_add_fusion.1), channel_id=1, source_target_pairs={{0,64},{64,0},{128,192},{192,128},{1,65},{65,1},{129,193},{193,129... | collective-permute-start | bytes 196616 | tf_op jit(solution)/shard_map/ppermute | solution.py:493
  20.7 11.5 %copy-start.6 = (f32[128,64]{1,0:T(8,128)S(1)}, f32[128,64]{1,0:T(8,128)}, u32[]{:S(2)}) copy-start(f32[128,64]{1,0:T(8,128)} %constant.99.clone.refs_11_) | copy-start | bytes 98308
  20.8 11.4 %copy-start.3 = (f32[64,512]{1,0:T(8,128)S(1)}, f32[64,512]{1,0:T(8,128)}, u32[]{:S(2)}) copy-start(f32[64,512]{1,0:T(8,128)} %constant.92.clone.refs_4_) | copy-start | bytes 393220
  20.8 11.5 %copy-start.4 = (f32[128,256]{1,0:T(8,128)S(1)}, f32[128,256]{1,0:T(8,128)}, u32[]{:S(2)}) copy-start(f32[128,256]{1,0:T(8,128)} %constant.95.clone.refs_7_) | copy-start | bytes 393220
  24.1 8.1 %collective-permute-start.2 = (s32[4,16,512]{2,1,0:T(8,128)S(1)}, s32[4,16,512]{2,1,0:T(8,128)S(1)}, u32[]{:S(2)}, u32[]{:S(2)}) collective-permute-start(s32[4,16,512]{2,1,0:T(8,128)S(1)} %pad_add_fusion), channel_id=1, source_target_pairs={{0,192},{64,128},{128,64},{192,0},{1,193},{65,129},{129,65},{193,1... | collective-permute-start | bytes 393224 | tf_op jit(solution)/shard_map/ppermute | solution.py:496
  37.7 13.0 %all-to-all-start.1 = ((f32[8,40,128]{2,1,0:T(8,128)}), f32[8,40,128]{2,1,0:T(8,128)S(1)}, u32[]{:S(2)}, u32[]{:S(2)}) async-start(f32[8,40,128]{2,1,0:T(8,128)} %shard_map.226), calls=%async_computation.1 | async-start | bytes 327680 | tf_op jit(solution)/shard_map/all_to_all | solution.py:480
  51.4 15.1 %copy-start.2 = (f32[128,512]{1,0:T(8,128)S(1)}, f32[128,512]{1,0:T(8,128)}, u32[]{:S(2)}) copy-start(f32[128,512]{1,0:T(8,128)} %constant.103.clone.refs_4_) | copy-start | bytes 786436
  51.4 15.1 %all-to-all-start.2 = ((f32[8,40,128]{2,1,0:T(8,128)}), f32[8,40,128]{2,1,0:T(8,128)S(1)}, u32[]{:S(2)}, u32[]{:S(2)}) async-start(f32[8,40,128]{2,1,0:T(8,128)} %shard_map.227), calls=%async_computation.2 | async-start | bytes 327680 | tf_op jit(solution)/shard_map/all_to_all | solution.py:480
  64.6 1.9 %copy-start.10 = (f32[1,512]{1,0:T(1,128)S(1)}, f32[1,512]{1,0:T(1,128)}, u32[]{:S(2)}) copy-start(f32[1,512]{1,0:T(1,128)} %constant.104.clone.refs_5_) | copy-start | bytes 6148

commit v2 on v1

--- a/solution.py
+++ b/solution.py
@@ -30,9 +30,9 @@
 NEAR = 8
 STEP = MC // BLOCKS
 LINES = ROWS + 1
-ROW_ORDER = None
+ROW_ORDER = [(k + 12) % 32 for k in range(32)]
 Y_ORDER = [4, 5, 6, 7, 0, 1, 2, 3]
-Z_ORDER = [4, 5, 6, 7, 0, 1, 2, 3]
+Z_ORDER = [5, 6, 7, 0, 1, 2, 3, 4]
 UNIT = 1.0 / math.sqrt(NR * NC)
 
 
@@ -72,10 +72,11 @@
 
 def band_tables():
     frequency = np.arange(KR) - KR // 2
-    rows = np.concatenate(wave(frequency, np.arange(NR), NR)) * (UNIT * UNIT)
+    heard_rows = (np.array(ROW_ORDER)[:, None] * ROWS + np.arange(ROWS)).reshape(-1)
+    rows = np.concatenate(wave(frequency, heard_rows, NR)) * (UNIT * UNIT)
     inner = np.zeros((2 * KR, KC))
     inner[:, :ROWS] = np.concatenate(wave(frequency, np.arange(ROWS), NR)) * (UNIT * UNIT)
-    outer = np.concatenate(wave(frequency, np.arange(ROW_BLOCKS) * ROWS, NR))
+    outer = np.concatenate(wave(frequency, np.array(ROW_ORDER) * ROWS, NR))
     return f32(rows), f32(inner), f32(outer)
 
 

time: 68.2 us -> 65.8 us (0.965)
  starting transfers between devices: 40.3 us -> 37.3 us
    all_to_all x3, starting transfers between devices: 33.1 us -> 30.1 us  [swap(): lax.all_to_all(values, axis, 0, 0, axis_index_groups=groups, tiled=True)]
where the time goes in v2:
time: 65.8 us; the launch traced here: 65.2 us
  starting transfers between devices  37.3 us (57%)
  waiting for transfers between devices  14.9 us (23%)
  Pallas kernels  9.88 us (15%)
  local copies, waits for them, and re-layouts  2.28 us (3%)
    all_to_all x3, starting transfers between devices, swap(): lax.all_to_all(values, axis, 0, 0, axis_index_groups=groups, tiled=True)  30.1 us
    pallas_call x3, Pallas kernels, call(): pl.pallas_call(body, in_specs=[SMEM] * len(scalars) + [VMEM] * len(arrays...  7.14 us
    all_to_all x3, waiting for transfers between devices, swap(): lax.all_to_all(values, axis, 0, 0, axis_index_groups=groups, tiled=True)  6.55 us
    ppermute x1, waiting for transfers between devices, local(): third = lax.ppermute(four, 'x', [(i, 3 - i) for i in range(4)])  5.08 us
    ppermute x1, waiting for transfers between devices, local(): second = lax.ppermute(two, 'x', [(i, i ^ 1) for i in range(4)])  3.29 us
    ppermute x1, starting transfers between devices, local(): second = lax.ppermute(two, 'x', [(i, i ^ 1) for i in range(4)])  2.87 us
    pallas_call x1, Pallas kernels, columns_part(): pl.pallas_call(kernel, grid_spec=pltpu.PrefetchScalarGridSpec(num_scalar_...  2.74 us
    ppermute x1, starting transfers between devices, local(): third = lax.ppermute(four, 'x', [(i, 3 - i) for i in range(4)])  2.41 us
  transfers between devices with their start and end apart: 6, of which 4 were waited for; matrix products, arithmetic and copies ran while one was open for 4% of the time, Pallas kernels for 4%

profile of v2, /device:TPU:6, one launch (start us, length us, event | category | flops | bytes accessed | tf_op | source)
XLA Modules:
  0.0 65.2 jit_solution(8467448354821299625)
XLA Ops:
  0.0 1.9 %collective-permute-start = (s32[16,512]{1,0:T(8,128)}, s32[16,512]{1,0:T(8,128)S(1)}, u32[]{:S(2)}, u32[]{:S(2)}) collective-permute-start(s32[16,512]{1,0:T(8,128)} %param.25), channel_id=1, source_target_pairs={{0,32},{32,0},{1,33},{33,1},{2,34},{34,2},{3,35},{35,3},{4,36},{36... | collective-permute-start | bytes 98312 | tf_op jit(solution)/shard_map/ppermute | solution.py:491
  1.9 0.0 copy-start.11
  1.9 0.0 copy-start.1
  1.9 0.0 copy-start.8
  2.0 2.7 %columns_part.1 = (f32[544,128]{1,0:T(8,128)}, f32[32,64]{1,0:T(8,128)S(1)}) custom-call(s32[1]{0:T(128)} %bitcast.8.place, f32[16,8192]{1,0:T(8,128)} %mask_ref.1, f32[32,32,64]{2,1,0:T(8,128)} %constant.87.clone.turn_ref, f32[136,512]{1,0:T(8,128)} %constant.88.clone.refs_0_, f32[16,128]{1,0:T(8,128)} %constant.89.clone.refs_1_, ...), custom_call_target="tpu_custom_call" | custom-call | tf_op jit(solution)/shard_map/columns_part/pallas_call | solution.py:383
  4.7 0.0 copy-start
  4.7 0.0 copy-start.7
  4.7 13.7 %all-to-all-start = ((f32[32,1,2176]{2,1,0:T(1,128)}), f32[32,1,2176]{2,1,0:T(1,128)S(1)}, u32[]{:S(2)}, u32[]{:S(2)}) async-start(f32[32,1,2176]{2,1,0:T(1,128)} %bitcast.9), calls=%async_computation | async-start | bytes 557056 | tf_op jit(solution)/shard_map/all_to_all | solution.py:481
  18.4 0.0 collective-permute-done
  18.5 0.0 copy-done.11
  18.5 0.0 copy-start.5
  18.5 0.0 copy-start.9
  18.5 2.9 %collective-permute-start.1 = (s32[2,16,512]{2,1,0:T(8,128)S(1)}, s32[2,16,512]{2,1,0:T(8,128)S(1)}, u32[]{:S(2)}, u32[]{:S(2)}) collective-permute-start(s32[2,16,512]{2,1,0:T(8,128)S(1)} %pad_add_fusion.1), channel_id=1, source_target_pairs={{0,64},{64,0},{128,192},{192,128},{1,65},{65,1},{129,193},{193,129... | collective-permute-start | bytes 196616 | tf_op jit(solution)/shard_map/ppermute | solution.py:494
  21.4 0.0 copy-start.6
  21.4 0.1 stack.44
  21.5 0.0 copy-start.3
  21.5 0.0 copy-start.4
  21.5 3.3 %collective-permute-done.1 = s32[2,16,512]{2,1,0:T(8,128)S(1)} collective-permute-done((s32[2,16,512]{2,1,0:T(8,128)S(1)}, s32[2,16,512]{2,1,0:T(8,128)S(1)}, u32[]{:S(2)}, u32[]{:S(2)}) %collective-permute-start.1) | collective-permute-done | bytes 65568 | tf_op jit(solution)/shard_map/ppermute | solution.py:494
  24.8 2.4 %collective-permute-start.2 = (s32[4,16,512]{2,1,0:T(8,128)S(1)}, s32[4,16,512]{2,1,0:T(8,128)S(1)}, u32[]{:S(2)}, u32[]{:S(2)}) collective-permute-start(s32[4,16,512]{2,1,0:T(8,128)S(1)} %pad_add_fusion), channel_id=1, source_target_pairs={{0,192},{64,128},{128,64},{192,0},{1,193},{65,129},{129,65},{193,1... | collective-permute-start | bytes 393224 | tf_op jit(solution)/shard_map/ppermute | solution.py:497
  27.2 0.6 multiply_add_fusion.shift_ref
  27.8 5.1 %collective-permute-done.2 = s32[4,16,512]{2,1,0:T(8,128)S(1)} collective-permute-done((s32[4,16,512]{2,1,0:T(8,128)S(1)}, s32[4,16,512]{2,1,0:T(8,128)S(1)}, u32[]{:S(2)}, u32[]{:S(2)}) %collective-permute-start.2) | collective-permute-done | bytes 131104 | tf_op jit(solution)/shard_map/ppermute | solution.py:497
  32.9 0.0 all-to-all-done
  32.9 0.0 copy-done.1
  32.9 0.0 copy-done.8
  32.9 0.0 copy-done
  32.9 0.0 copy-done.7
  32.9 0.0 copy-done.5
  32.9 0.0 copy-done.9
  32.9 0.0 copy-done.6
  32.9 0.0 copy-done.3
  33.0 0.0 copy-done.4
  33.0 5.4 %shard_map.226 = f32[8,40,128]{2,1,0:T(8,128)} custom-call(s32[8]{0:T(128)} %multiply_add_fusion.shift_ref, f32[16]{0:T(128)} %weight_ref.1, s32[16]{0:T(128)} %row_ref.1, s32[16]{0:T(128)} %col_ref.1, f32[544,128]{1,0:T(8,128)S(1)} %bitcast.22, s32[32,512]{1,0:T(8,128)S(1)} %bitcast.23, s32[32,512]{1,0:T(8,128)S(1)} %bitcast.24, s32[64,512]{1,0:T(8,128)S(1)} %bitcast.25, ...), custom_call_target="tpu_custom_call" | custom-call | tf_op jit(solution)/shard_map/pallas_call | solution.py:347
  38.3 7.2 %all-to-all-start.1 = ((f32[8,40,128]{2,1,0:T(8,128)}), f32[8,40,128]{2,1,0:T(8,128)S(1)}, u32[]{:S(2)}, u32[]{:S(2)}) async-start(f32[8,40,128]{2,1,0:T(8,128)} %shard_map.226), calls=%async_computation.1 | async-start | bytes 327680 | tf_op jit(solution)/shard_map/all_to_all | solution.py:481
  45.6 4.1 %all-to-all-done.1.in_ref = f32[8,40,128]{2,1,0:T(8,128)S(1)} async-done(((f32[8,40,128]{2,1,0:T(8,128)}), f32[8,40,128]{2,1,0:T(8,128)S(1)}, u32[]{:S(2)}, u32[]{:S(2)}) %all-to-all-start.1) | async-done | bytes 163872 | tf_op jit(solution)/shard_map/all_to_all | solution.py:481
  49.6 0.7 %shard_map.227 = f32[8,40,128]{2,1,0:T(8,128)} custom-call(f32[8,40,128]{2,1,0:T(8,128)S(1)} %all-to-all-done.1.in_ref), custom_call_target="tpu_custom_call" | custom-call | tf_op jit(solution)/shard_map/pallas_call | solution.py:347
  50.3 0.0 copy-start.2
  50.3 9.2 %all-to-all-start.2 = ((f32[8,40,128]{2,1,0:T(8,128)}), f32[8,40,128]{2,1,0:T(8,128)S(1)}, u32[]{:S(2)}, u32[]{:S(2)}) async-start(f32[8,40,128]{2,1,0:T(8,128)} %shard_map.227), calls=%async_computation.2 | async-start | bytes 327680 | tf_op jit(solution)/shard_map/all_to_all | solution.py:481
  59.5 0.7 %fusion = (f32[1,128]{1,0:T(1,128)S(1)}, f32[1,128]{1,0:T(1,128)S(1)}) fusion(f32[16,1,128]{2,1,0:T(1,128)} %constant.101.clone, s32[]{:T(128)S(6)} %select_n.14, f32[16,1,128]{2,1,0:T(1,128)} %constant.102.clone), kind=kLoop, calls=%fused_computation.6 | loop fusion | bytes 2052 | tf_op jit(solution)/shard_map/jit(dynamic_index_in_dim)/squeeze | solution.py:360
  60.1 0.7 %dynamic-slice_bitcast_fusion.refs_1_ = f32[16,128]{1,0:T(8,128)S(1)} fusion(f32[32,16,128]{2,1,0:T(8,128)} %constant.100.clone, s32[]{:T(128)S(6)} %select_n.13), kind=kLoop, calls=%fused_computation.2 | loop fusion | bytes 16388 | tf_op jit(solution)/shard_map/jit(dynamic_index_in_dim)/squeeze | solution.py:360
  60.8 0.8 %constant_dynamic-slice_fusion.2.refs_0_ = f32[16,512]{1,0:T(8,128)S(1)} fusion(f32[16,8192]{1,0:T(8,128)} %mask_ref.1, s32[]{:T(128)S(6)} %select_n.12), kind=kLoop, calls=%fused_computation.5 | loop fusion | bytes 65540 | tf_op jit(solution)/shard_map/dynamic_slice | solution.py:460
  61.6 0.0 copy-start.10
  61.6 2.5 %all-to-all-done.2.in_ref = f32[8,40,128]{2,1,0:T(8,128)S(1)} async-done(((f32[8,40,128]{2,1,0:T(8,128)}), f32[8,40,128]{2,1,0:T(8,128)S(1)}, u32[]{:S(2)}, u32[]{:S(2)}) %all-to-all-start.2) | async-done | bytes 163872 | tf_op jit(solution)/shard_map/all_to_all | solution.py:481
  64.1 0.0 copy-done.2
  64.1 0.0 copy-done.10
  64.1 1.1 %shard_map.228 = f32[16,512]{1,0:T(8,128)} custom-call(f32[8,40,128]{2,1,0:T(8,128)S(1)} %all-to-all-done.2.in_ref, f32[16,512]{1,0:T(8,128)S(1)} %constant_dynamic-slice_fusion.2.refs_0_, f32[16,128]{1,0:T(8,128)S(1)} %dynamic-slice_bitcast_fusion.refs_1_, f32[1,128]{1,0:T(1,128)S(1)} %get-tuple-element.9.refs_2_, f32[1,128]{1,0:T(1,128)S(1)} %get-tuple-element.10.refs_3_, ...), custom_call_target="tpu_custom_call" | custom-call | tf_op jit(solution)/shard_map/pallas_call | solution.py:347
  (2 shorter events, 0.0 us)
Async XLA Ops:
  0.0 18.4 %collective-permute-start = (s32[16,512]{1,0:T(8,128)}, s32[16,512]{1,0:T(8,128)S(1)}, u32[]{:S(2)}, u32[]{:S(2)}) collective-permute-start(s32[16,512]{1,0:T(8,128)} %param.25), channel_id=1, source_target_pairs={{0,32},{32,0},{1,33},{33,1},{2,34},{34,2},{3,35},{35,3},{4,36},{36... | collective-permute-start | bytes 98312 | tf_op jit(solution)/shard_map/ppermute | solution.py:491
  1.9 16.5 %copy-start.11 = (s32[16,512]{1,0:T(8,128)S(1)}, s32[16,512]{1,0:T(8,128)}, u32[]{:S(2)}) copy-start(s32[16,512]{1,0:T(8,128)} %param.25) | copy-start | bytes 98308
  1.9 31.0 %copy-start.1 = (f32[256,512]{1,0:T(8,128)S(1)}, f32[256,512]{1,0:T(8,128)}, u32[]{:S(2)}) copy-start(f32[256,512]{1,0:T(8,128)} %constant.97.clone.refs_9_) | copy-start | bytes 1572868
  1.9 30.9 %copy-start.8 = (f32[64,32]{1,0:T(8,128)S(1)}, f32[64,32]{1,0:T(8,128)}, u32[]{:S(2)}) copy-start(f32[64,32]{1,0:T(8,128)} %constant.94.clone.refs_6_) | copy-start | bytes 24580
  4.7 28.2 %copy-start = (f32[256,512]{1,0:T(8,128)S(1)}, f32[256,512]{1,0:T(8,128)}, u32[]{:S(2)}) copy-start(f32[256,512]{1,0:T(8,128)} %constant.96.clone.refs_8_) | copy-start | bytes 1572868
  4.7 28.2 %copy-start.7 = (f32[64,128]{1,0:T(8,128)S(1)}, f32[64,128]{1,0:T(8,128)}, u32[]{:S(2)}) copy-start(f32[64,128]{1,0:T(8,128)} %constant.93.clone.refs_5_) | copy-start | bytes 98308
  4.7 28.2 %all-to-all-start = ((f32[32,1,2176]{2,1,0:T(1,128)}), f32[32,1,2176]{2,1,0:T(1,128)S(1)}, u32[]{:S(2)}, u32[]{:S(2)}) async-start(f32[32,1,2176]{2,1,0:T(1,128)} %bitcast.9), calls=%async_computation | async-start | bytes 557056 | tf_op jit(solution)/shard_map/all_to_all | solution.py:481
  18.5 14.5 %copy-start.5 = (f32[128,256]{1,0:T(8,128)S(1)}, f32[128,256]{1,0:T(8,128)}, u32[]{:S(2)}) copy-start(f32[128,256]{1,0:T(8,128)} %constant.98.clone.refs_10_) | copy-start | bytes 393220
  18.5 14.4 %copy-start.9 = (f32[8,128]{1,0:T(8,128)S(1)}, f32[8,128]{1,0:T(8,128)}, u32[]{:S(2)}) copy-start(f32[8,128]{1,0:T(8,128)} %constant.91.clone.refs_3_.refs_12_) | copy-start | bytes 12292
  18.5 6.3 %collective-permute-start.1 = (s32[2,16,512]{2,1,0:T(8,128)S(1)}, s32[2,16,512]{2,1,0:T(8,128)S(1)}, u32[]{:S(2)}, u32[]{:S(2)}) collective-permute-start(s32[2,16,512]{2,1,0:T(8,128)S(1)} %pad_add_fusion.1), channel_id=1, source_target_pairs={{0,64},{64,0},{128,192},{192,128},{1,65},{65,1},{129,193},{193,129... | collective-permute-start | bytes 196616 | tf_op jit(solution)/shard_map/ppermute | solution.py:494
  21.4 11.5 %copy-start.6 = (f32[128,64]{1,0:T(8,128)S(1)}, f32[128,64]{1,0:T(8,128)}, u32[]{:S(2)}) copy-start(f32[128,64]{1,0:T(8,128)} %constant.99.clone.refs_11_) | copy-start | bytes 98308
  21.5 11.4 %copy-start.3 = (f32[64,512]{1,0:T(8,128)S(1)}, f32[64,512]{1,0:T(8,128)}, u32[]{:S(2)}) copy-start(f32[64,512]{1,0:T(8,128)} %constant.92.clone.refs_4_) | copy-start | bytes 393220
  21.5 11.5 %copy-start.4 = (f32[128,256]{1,0:T(8,128)S(1)}, f32[128,256]{1,0:T(8,128)}, u32[]{:S(2)}) copy-start(f32[128,256]{1,0:T(8,128)} %constant.95.clone.refs_7_) | copy-start | bytes 393220
  24.8 8.1 %collective-permute-start.2 = (s32[4,16,512]{2,1,0:T(8,128)S(1)}, s32[4,16,512]{2,1,0:T(8,128)S(1)}, u32[]{:S(2)}, u32[]{:S(2)}) collective-permute-start(s32[4,16,512]{2,1,0:T(8,128)S(1)} %pad_add_fusion), channel_id=1, source_target_pairs={{0,192},{64,128},{128,64},{192,0},{1,193},{65,129},{129,65},{193,1... | collective-permute-start | bytes 393224 | tf_op jit(solution)/shard_map/ppermute | solution.py:497
  38.3 11.3 %all-to-all-start.1 = ((f32[8,40,128]{2,1,0:T(8,128)}), f32[8,40,128]{2,1,0:T(8,128)S(1)}, u32[]{:S(2)}, u32[]{:S(2)}) async-start(f32[8,40,128]{2,1,0:T(8,128)} %shard_map.226), calls=%async_computation.1 | async-start | bytes 327680 | tf_op jit(solution)/shard_map/all_to_all | solution.py:481
  50.3 13.8 %copy-start.2 = (f32[128,512]{1,0:T(8,128)S(1)}, f32[128,512]{1,0:T(8,128)}, u32[]{:S(2)}) copy-start(f32[128,512]{1,0:T(8,128)} %constant.103.clone.refs_4_) | copy-start | bytes 786436
  50.3 13.8 %all-to-all-start.2 = ((f32[8,40,128]{2,1,0:T(8,128)}), f32[8,40,128]{2,1,0:T(8,128)S(1)}, u32[]{:S(2)}, u32[]{:S(2)}) async-start(f32[8,40,128]{2,1,0:T(8,128)} %shard_map.227), calls=%async_computation.2 | async-start | bytes 327680 | tf_op jit(solution)/shard_map/all_to_all | solution.py:481
  61.6 2.5 %copy-start.10 = (f32[1,512]{1,0:T(1,128)S(1)}, f32[1,512]{1,0:T(1,128)}, u32[]{:S(2)}) copy-start(f32[1,512]{1,0:T(1,128)} %constant.104.clone.refs_5_) | copy-start | bytes 6148
